TPU v7x, 256 devices: a whole 4x4x8 slice. The times are simulated.
256 devices in a mesh: blk: 32 (over z_hi, x, core), grp: 8 (over z_lo, y).
Axes of the slice: x: 4, y: 4, z: 8 (z_hi: 4, z_lo: 2; z = z_hi * 2 + z_lo), core: 2. Of those that a mesh axis runs over, the one named last changes fastest.
Arguments:
- inv_tiles: bfloat16 [64, 64, 512, 512], P(None, 'grp', 'blk'), may hold values from -6 to 6
- factor: bfloat16 [8, 16, 512, 512], P('grp', None, 'blk'), may hold values from -0.0625 to 0.0625
- diag_inv_factor: float32 [8, 512, 512], P('grp', 'blk'), may hold values from -6 to 6
- structure: int32 [8, 16], replicated, may hold values from 0 to 63, as said below
Outputs:
- offdiag_inv: bfloat16 [8, 16, 512, 512], P('grp', None, 'blk')
- diag_inv: float32 [8, 512, 512], P('grp', 'blk')
Inputs may be any that keep to these rules, and one draw needn't show every extreme that they name: `structure`: each row lists 16 distinct ancestor blocks in ascending order, exactly 2 in each run of 8 blocks that starts at a multiple of 8; block 63 is listed in every row.
All inputs are finite; a program needn't handle non-finite values.
Results may differ from a plain program's by a relative error of at most 0.018.
Values may be sent and summed in bfloat16 or wider, within the bound.
A program may use at most 128 MiB of HBM per device.

v0:
```python
import jax
import jax.numpy as jnp
from jax import lax
from jax.sharding import PartitionSpec as P


def split_up(shard, dim, count):
    dims = shard.shape
    tiles = shard.reshape(*dims[:dim], count, dims[dim] // count, *dims[dim + 1 :])
    return jnp.moveaxis(tiles, dim, 0)


def sum_at_owner(shard, axis, dim):
    count = lax.axis_size(axis)
    tiles = lax.all_to_all(split_up(shard, dim, count), axis, 0, 0, tiled=True)
    return jnp.sum(tiles.astype(jnp.float32), axis=0)


def on_device(inv_tiles, factor, diag_inv_factor, structure):
    grp_count = lax.axis_size("grp")
    grp_index = lax.axis_index("grp")
    col_local = inv_tiles.shape[1]
    width = inv_tiles.shape[3]
    own_count = factor.shape[0]
    listed_count = factor.shape[1]
    slab_rows = factor.shape[2]
    per_group = listed_count // grp_count
    node_total = own_count * grp_count
    grouped = factor.reshape(own_count, grp_count, per_group, slab_rows, width)
    received = lax.all_to_all(grouped, "grp", split_axis=1, concat_axis=0, tiled=True)
    received = received.reshape(node_total, per_group, slab_rows, width)
    readers = lax.all_gather(received, "blk", axis=2, tiled=True)
    col_base = grp_index * col_local
    local_cols = lax.dynamic_slice_in_dim(structure, grp_index * per_group, per_group, 1) - col_base
    selected = inv_tiles[structure[:, :, None], local_cols[:, None, :]]
    summed = sum_at_owner(
        jnp.einsum(
            "crjxy,cjyz->crxz", selected, readers, preferred_element_type=jnp.float32
        ).astype(jnp.bfloat16),
        "grp",
        0,
    )
    offdiag = (-summed).astype(jnp.bfloat16)
    correction = sum_at_owner(
        jnp.einsum("krxy,krxz->ykz", factor, offdiag, preferred_element_type=jnp.float32).astype(
            jnp.bfloat16
        ),
        "blk",
        0,
    )
    diag_inv = diag_inv_factor - jnp.transpose(correction, (1, 0, 2))
    return (offdiag, diag_inv)


def solution(mesh):
    return jax.shard_map(
        on_device,
        mesh=mesh,
        in_specs=(
            P(None, "grp", "blk", None),
            P("grp", None, "blk", None),
            P("grp", "blk", None),
            P(),
        ),
        out_specs=(P("grp", None, "blk", None), P("grp", "blk", None)),
        check_vma=False,
    )
```

profile of v0, /device:TPU:1, one launch (start us, length us, event | category | flops | bytes accessed | tf_op | source)
XLA Modules:
  0.0 173.3 jit_solution(4277369298304297157)
XLA Ops:
  7.2 0.0 all-gather.3.cloned.1.call-start
  7.2 12.6 %all_to_all.19 = bf16[1,8,2,16,512]{4,3,2,0,1:T(8,128)(2,1)} all-to-all(bf16[1,8,2,16,512]{4,3,2,0,1:T(8,128)(2,1)} %bitcast.46), channel_id=1, replica_groups=mesh['blk'=32,'grp'=8] {'grp'}, dimensions={1} | all-to-all | bytes 524288 | tf_op jit(solution)/shard_map/all_to_all | solution.py:30
  19.8 0.0 all-gather.3.cloned.1.call-update
  19.8 0.8 fusion.13
  20.6 0.7 fusion.11
  21.3 0.1 broadcast_or_fusion
  21.4 0.1 reshape.63
  21.5 6.5 %gather_fusion = bf16[256,16,512]{2,1,0:T(8,128)(2,1)} fusion(bf16[64,8,16,512]{3,2,1,0:T(8,128)(2,1)} %param.4, s32[256]{0:T(256)S(1)} %reshape.63), kind=kCustom, calls=%fused_computation | custom fusion | bytes 8390656 | tf_op jit(solution)/shard_map/gather | solution.py:35
  28.0 69.7 %all-gather.3.cloned.1.call-done = bf16[1,8,2,512,512]{4,3,2,1,0:T(8,128)(2,1)} async-done(((bf16[1,8,2,16,512]{4,3,2,1,0:T(8,128)(2,1)}), bf16[1,8,2,512,512]{4,3,2,1,0:T(8,128)(2,1)}) %all-gather.3.cloned.1.call-update) | async-done | bytes 8388624 | tf_op jit(solution)/shard_map/all_gather | solution.py:32
  97.7 7.0 %fusion.4 = bf16[8,1,16,16,512]{4,3,2,1,0:T(8,128)(2,1)S(1)} fusion(bf16[8,16,2,16,512]{4,3,2,1,0:T(8,128)(2,1)} %bitcast.45, bf16[1,8,2,512,512]{4,3,2,1,0:T(8,128)(2,1)} %all-gather.3.cloned.1.call-done), kind=kOutput, calls=%fused_computation.5 | convolution fusion | flops 2148532224 | bytes 14680064 | tf_op jit(solution)/shard_map/crjxy,cjyz->crxz/dot_general | solution.py:37
  104.7 0.0 copy-start
  104.7 33.1 %all_to_all.20 = bf16[8,1,16,16,512]{4,3,2,1,0:T(8,128)(2,1)S(1)} all-to-all(bf16[8,1,16,16,512]{4,3,2,1,0:T(8,128)(2,1)S(1)} %fusion.4), channel_id=1, replica_groups=mesh['blk'=32,'grp'=8] {'grp'}, dimensions={0} | all-to-all | bytes 4194304 | tf_op jit(solution)/shard_map/all_to_all | solution.py:15
  137.8 0.0 copy-start.1
  137.8 0.4 convert_reduce_fusion
  138.1 0.0 copy-done
  138.1 1.1 fusion.7
  139.3 8.1 %all-to-all-start.2 = ((bf16[32,16,1,512]{3,1,2,0:T(8,128)(2,1)}), bf16[32,16,1,512]{3,1,2,0:T(8,128)(2,1)S(1)}, u32[]{:S(2)}, u32[]{:S(2)}) async-start(bf16[32,16,1,512]{3,1,2,0:T(8,128)(2,1)} %bitcast.16), calls=%async_computation.2 | async-start | bytes 1048576 | tf_op jit(solution)/shard_map/all_to_all | solution.py:15
  147.4 0.7 fusion.9
  148.1 17.6 %all-to-all-done.2 = bf16[32,16,1,512]{3,1,2,0:T(8,128)(2,1)S(1)} async-done(((bf16[32,16,1,512]{3,1,2,0:T(8,128)(2,1)}), bf16[32,16,1,512]{3,1,2,0:T(8,128)(2,1)S(1)}, u32[]{:S(2)}, u32[]{:S(2)}) %all-to-all-start.2) | async-done | bytes 524320 | tf_op jit(solution)/shard_map/all_to_all | solution.py:15
  165.7 0.1 convert_reduce_fusion.1
  165.8 0.0 copy-done.1
  165.8 0.6 bitcast_subtract_fusion
Async XLA Ops:
  7.2 90.5 %all-gather.3.cloned.1.call-start = ((), (), s32[]{:S(2)}) async-start(), calls=%async_computation.3 | async-start | bytes 8650752 | tf_op jit(solution)/shard_map/all_gather | solution.py:32
  104.7 33.4 %copy-start = (bf16[1,16,16,512]{3,2,1,0:T(8,128)(2,1)S(1)}, bf16[1,16,16,512]{3,2,1,0:T(8,128)(2,1)}, u32[]{:S(2)}) copy-start(bf16[1,16,16,512]{3,2,1,0:T(8,128)(2,1)} %param.5) | copy-start | bytes 786436
  137.8 28.1 %copy-start.1 = (f32[1,16,512]{2,1,0:T(8,128)S(1)}, f32[1,16,512]{2,1,0:T(8,128)}, u32[]{:S(2)}) copy-start(f32[1,16,512]{2,1,0:T(8,128)} %param.6) | copy-start | bytes 98308
  139.3 26.5 %all-to-all-start.2 = ((bf16[32,16,1,512]{3,1,2,0:T(8,128)(2,1)}), bf16[32,16,1,512]{3,1,2,0:T(8,128)(2,1)S(1)}, u32[]{:S(2)}, u32[]{:S(2)}) async-start(bf16[32,16,1,512]{3,1,2,0:T(8,128)(2,1)} %bitcast.16), calls=%async_computation.2 | async-start | bytes 1048576 | tf_op jit(solution)/shard_map/all_to_all | solution.py:15
Sparse Core Ops, SparseCore 0:
  19.9 77.6 all-gather.2
where the time goes:
time: 174 us; the launch traced here: 173 us
  waiting for transfers between devices  87.3 us (50%)
  blocking collectives  45.7 us (26%)
  between operations  14.1 us (8%)
  matrix products  8.13 us (5%)
  starting transfers between devices  8.12 us (5%)
  local copies, waits for them, and re-layouts  6.66 us (4%)
  other arithmetic  3.35 us (2%)
    all_gather x1, waiting for transfers between devices, on_device(): readers = lax.all_gather(received, 'blk', axis=2, tiled=True)  69.7 us
    all_to_all x1, blocking collectives, sum_at_owner(): tiles = lax.all_to_all(split_up(shard, dim, count), axis, 0, 0, tiled=True)  33.1 us
    all_to_all x1, waiting for transfers between devices, sum_at_owner(): tiles = lax.all_to_all(split_up(shard, dim, count), axis, 0, 0, tiled=True)  17.6 us
    all_to_all x1, blocking collectives, on_device(): lax.all_to_all(grouped, 'grp', split_axis=1, concat_axis=0, tiled=True)  12.6 us
    all_to_all x1, starting transfers between devices, sum_at_owner(): tiles = lax.all_to_all(split_up(shard, dim, count), axis, 0, 0, tiled=True)  8.09 us
    dot_general x1, matrix products, on_device(): jnp.einsum('crjxy,cjyz->crxz', selected, readers, preferred_element_type=...  6.99 us
    gather x1, local copies, waits for them, and re-layouts, on_device(): selected = inv_tiles[structure[:, :, None], local_cols[:, None, :]]  6.51 us
  transfers between devices with their start and end apart: 2, of which 2 were waited for; matrix products, arithmetic and copies ran while one was open for 5% of the time, Pallas kernels for 0%

commit v1 on v0

--- a/solution.py
+++ b/solution.py
@@ -29,7 +29,8 @@
     grouped = factor.reshape(own_count, grp_count, per_group, slab_rows, width)
     received = lax.all_to_all(grouped, "grp", split_axis=1, concat_axis=0, tiled=True)
     received = received.reshape(node_total, per_group, slab_rows, width)
-    readers = lax.all_gather(received, "blk", axis=2, tiled=True)
+    stack = jnp.stack([received] * lax.axis_size("blk"))
+    readers = jnp.concatenate(lax.all_to_all(stack, "blk", 0, 0), axis=2)
     col_base = grp_index * col_local
     local_cols = lax.dynamic_slice_in_dim(structure, grp_index * per_group, per_group, 1) - col_base
     selected = inv_tiles[structure[:, :, None], local_cols[:, None, :]]

time: 174 us -> 289 us (1.66)
  waiting for transfers between devices: 87.3 us -> 195 us
  starting transfers between devices: 8.12 us -> 23 us
  between operations: 14.1 us -> 0.71 us
  local copies, waits for them, and re-layouts: 6.66 us -> 19.2 us
  blocking collectives: 45.7 us -> 41.7 us
    all_to_all x0 -> x1, waiting for transfers between devices: none -> 178 us  [on_device(): readers = jnp.concatenate(lax.all_to_all(stack, 'blk', 0, 0), axis=2)]
    all_gather x1 -> x0, waiting for transfers between devices: 69.7 us -> none  [on_device(): readers = lax.all_gather(received, 'blk', axis=2, tiled=True)]
    all_to_all x0 -> x1, starting transfers between devices: none -> 12.4 us  [on_device(): readers = jnp.concatenate(lax.all_to_all(stack, 'blk', 0, 0), axis=2)]
    reshape x0 -> x1, local copies, waits for them, and re-layouts: none -> 8.22 us  [on_device(): readers = jnp.concatenate(lax.all_to_all(stack, 'blk', 0, 0), axis=2)]
    another operation x0 -> x1, local copies, waits for them, and re-layouts: none -> 4.3 us  [on_device(): stack = jnp.stack([received] * lax.axis_size('blk'))]
    all_to_all x1, blocking collectives: 33.1 us -> 29.2 us  [sum_at_owner(): tiles = lax.all_to_all(split_up(shard, dim, count), axis, 0, 0, tiled=True)]
  transfers between devices with their start and end apart: 2 -> 2, of which waited for: 2 -> 2; matrix products, arithmetic and copies ran while one was open for 5% -> 3% of each run, Pallas kernels for 0% -> 0%
where the time goes in v1:
time: 289 us
  waiting for transfers between devices  195 us (67%)
  blocking collectives  41.7 us (14%)
  starting transfers between devices  23 us (8%)
  local copies, waits for them, and re-layouts  19.2 us (7%)
  matrix products  6.86 us (2%)
    all_to_all x1, waiting for transfers between devices, on_device(): readers = jnp.concatenate(lax.all_to_all(stack, 'blk', 0, 0), axis=2)  178 us
    all_to_all x1, blocking collectives, sum_at_owner(): tiles = lax.all_to_all(split_up(shard, dim, count), axis, 0, 0, tiled=True)  29.2 us
    all_to_all x1, waiting for transfers between devices, sum_at_owner(): tiles = lax.all_to_all(split_up(shard, dim, count), axis, 0, 0, tiled=True)  17.6 us
    all_to_all x1, blocking collectives, on_device(): lax.all_to_all(grouped, 'grp', split_axis=1, concat_axis=0, tiled=True)  12.5 us
    all_to_all x1, starting transfers between devices, on_device(): readers = jnp.concatenate(lax.all_to_all(stack, 'blk', 0, 0), axis=2)  12.4 us
    all_to_all x1, starting transfers between devices, sum_at_owner(): tiles = lax.all_to_all(split_up(shard, dim, count), axis, 0, 0, tiled=True)  10.5 us
    reshape x1, local copies, waits for them, and re-layouts, on_device(): readers = jnp.concatenate(lax.all_to_all(stack, 'blk', 0, 0), axis=2)  8.22 us
    gather x1, local copies, waits for them, and re-layouts, on_device(): selected = inv_tiles[structure[:, :, None], local_cols[:, None, :]]  6.48 us
  transfers between devices with their start and end apart: 2, of which 2 were waited for; matrix products, arithmetic and copies ran while one was open for 3% of the time, Pallas kernels for 0%

profile of v1, /device:TPU:1, one launch (start us, length us, event | category | flops | bytes accessed | tf_op | source)
XLA Modules:
  0.0 288.8 jit_solution(210310976270969708)
XLA Ops:
  0.6 12.5 %all_to_all.24 = bf16[1,8,2,16,512]{4,3,2,0,1:T(8,128)(2,1)S(1)} all-to-all(bf16[1,8,2,16,512]{4,3,2,0,1:T(8,128)(2,1)} %bitcast.44), channel_id=1, replica_groups=mesh['blk'=32,'grp'=8] {'grp'}, dimensions={1} | all-to-all | bytes 524288 | tf_op jit(solution)/shard_map/all_to_all | solution.py:30
  13.1 4.3 %stack.3 = bf16[32,8,2,16,512]{4,3,2,1,0:T(8,128)(2,1)} broadcast(bf16[8,2,16,512]{3,2,1,0:T(8,128)(2,1)S(1)} %bitcast.45), dimensions={1,2,3,4} | broadcast | bytes 8650752 | tf_op jit(solution)/shard_map/stack | solution.py:32
  17.4 0.0 copy-start.3
  17.4 12.4 %all-to-all-start.1 = ((bf16[32,8,2,16,512]{4,3,2,1,0:T(8,128)(2,1)}), bf16[32,8,2,16,512]{4,3,2,1,0:T(8,128)(2,1)}, u32[]{:S(2)}, u32[]{:S(2)}) async-start(bf16[32,8,2,16,512]{4,3,2,1,0:T(8,128)(2,1)} %stack.3), calls=%async_computation.1 | async-start | bytes 16777216 | tf_op jit(solution)/shard_map/all_to_all | solution.py:33
  29.9 0.0 copy-done.3
  29.9 0.1 fusion.7
  30.0 0.1 broadcast_or_fusion
  30.1 0.1 reshape.69
  30.2 6.5 %gather_fusion = bf16[256,16,512]{2,1,0:T(8,128)(2,1)} fusion(bf16[64,8,16,512]{3,2,1,0:T(8,128)(2,1)} %param.4, s32[256]{0:T(256)S(1)} %reshape.69), kind=kCustom, calls=%fused_computation | custom fusion | bytes 8390656 | tf_op jit(solution)/shard_map/gather | solution.py:36
  36.7 177.7 %all-to-all-done.1 = bf16[32,8,2,16,512]{4,3,2,1,0:T(8,128)(2,1)} async-done(((bf16[32,8,2,16,512]{4,3,2,1,0:T(8,128)(2,1)}), bf16[32,8,2,16,512]{4,3,2,1,0:T(8,128)(2,1)}, u32[]{:S(2)}, u32[]{:S(2)}) %all-to-all-start.1) | async-done | bytes 8388640 | tf_op jit(solution)/shard_map/all_to_all | solution.py:33
  214.4 0.0 copy-start
  214.4 8.2 %copy.6 = bf16[8,2,32,16,512]{4,3,2,1,0:T(8,128)(2,1)} copy(bf16[8,2,32,16,512]{4,3,1,0,2:T(8,128)(2,1)} %bitcast.3) | data formatting | bytes 16777216 | tf_op jit(solution)/shard_map/reshape | solution.py:33
  222.6 0.0 copy-done
  222.6 5.7 %fusion = bf16[8,1,16,16,512]{4,3,2,1,0:T(8,128)(2,1)S(1)} fusion(bf16[8,16,2,16,512]{4,3,2,1,0:T(8,128)(2,1)S(1)} %bitcast.43, bf16[8,2,512,512,1]{3,2,1,4,0:T(8,128)(2,1)} %bitcast.42), kind=kOutput, calls=%fused_computation.3 | convolution fusion | flops 2148532224 | bytes 14680064 | tf_op jit(solution)/shard_map/crjxy,cjyz->crxz/dot_general | solution.py:38
  228.4 0.0 copy-start.1
  228.4 29.2 %all_to_all.25 = bf16[8,1,16,16,512]{4,3,2,1,0:T(8,128)(2,1)S(1)} all-to-all(bf16[8,1,16,16,512]{4,3,2,1,0:T(8,128)(2,1)S(1)} %fusion), channel_id=1, replica_groups=mesh['blk'=32,'grp'=8] {'grp'}, dimensions={0} | all-to-all | bytes 4194304 | tf_op jit(solution)/shard_map/all_to_all | solution.py:15
  257.6 0.0 copy-start.2
  257.6 0.4 convert_reduce_fusion
  258.0 0.0 copy-done.1
  258.0 1.2 fusion.1
  259.1 10.5 %all-to-all-start.3 = ((bf16[32,16,1,512]{3,1,2,0:T(8,128)(2,1)}), bf16[32,16,1,512]{3,1,2,0:T(8,128)(2,1)S(1)}, u32[]{:S(2)}, u32[]{:S(2)}) async-start(bf16[32,16,1,512]{3,1,2,0:T(8,128)(2,1)} %bitcast.17), calls=%async_computation.3 | async-start | bytes 1048576 | tf_op jit(solution)/shard_map/all_to_all | solution.py:15
  269.7 0.7 fusion.3
  270.4 17.6 %all-to-all-done.3 = bf16[32,16,1,512]{3,1,2,0:T(8,128)(2,1)S(1)} async-done(((bf16[32,16,1,512]{3,1,2,0:T(8,128)(2,1)}), bf16[32,16,1,512]{3,1,2,0:T(8,128)(2,1)S(1)}, u32[]{:S(2)}, u32[]{:S(2)}) %all-to-all-start.3) | async-done | bytes 524320 | tf_op jit(solution)/shard_map/all_to_all | solution.py:15
  288.0 0.1 convert_reduce_fusion.1
  288.1 0.0 copy-done.2
  288.1 0.6 bitcast_subtract_fusion
  (1 shorter events, 0.0 us)
Async XLA Ops:
  17.4 12.5 %copy-start.3 = (s32[8,16]{1,0:T(8,128)S(1)}, s32[8,16]{1,0:T(8,128)}, u32[]{:S(2)}) copy-start(s32[8,16]{1,0:T(8,128)} %param.7) | copy-start | bytes 1540
  17.4 197.0 %all-to-all-start.1 = ((bf16[32,8,2,16,512]{4,3,2,1,0:T(8,128)(2,1)}), bf16[32,8,2,16,512]{4,3,2,1,0:T(8,128)(2,1)}, u32[]{:S(2)}, u32[]{:S(2)}) async-start(bf16[32,8,2,16,512]{4,3,2,1,0:T(8,128)(2,1)} %stack.3), calls=%async_computation.1 | async-start | bytes 16777216 | tf_op jit(solution)/shard_map/all_to_all | solution.py:33
  214.4 8.2 %copy-start = (bf16[256,16,512]{2,1,0:T(8,128)(2,1)S(1)}, bf16[256,16,512]{2,1,0:T(8,128)(2,1)}, u32[]{:S(2)}) copy-start(bf16[256,16,512]{2,1,0:T(8,128)(2,1)} %gather_fusion) | copy-start | bytes 12582916
  228.4 29.6 %copy-start.1 = (bf16[1,16,16,512]{3,2,1,0:T(8,128)(2,1)S(1)}, bf16[1,16,16,512]{3,2,1,0:T(8,128)(2,1)}, u32[]{:S(2)}) copy-start(bf16[1,16,16,512]{3,2,1,0:T(8,128)(2,1)} %param.5) | copy-start | bytes 786436
  257.6 30.5 %copy-start.2 = (f32[1,16,512]{2,1,0:T(8,128)S(1)}, f32[1,16,512]{2,1,0:T(8,128)}, u32[]{:S(2)}) copy-start(f32[1,16,512]{2,1,0:T(8,128)} %param.6) | copy-start | bytes 98308
  259.1 28.9 %all-to-all-start.3 = ((bf16[32,16,1,512]{3,1,2,0:T(8,128)(2,1)}), bf16[32,16,1,512]{3,1,2,0:T(8,128)(2,1)S(1)}, u32[]{:S(2)}, u32[]{:S(2)}) async-start(bf16[32,16,1,512]{3,1,2,0:T(8,128)(2,1)} %bitcast.17), calls=%async_computation.3 | async-start | bytes 1048576 | tf_op jit(solution)/shard_map/all_to_all | solution.py:15
